TPU v7x, 32 devices: a whole 2x2x4 slice. The times are simulated.
32 devices in a mesh: tm: 4 (over x, core), height: 8 (over z, y).
Axes of the slice: x: 2, y: 2, z: 4, core: 2. Of those that a mesh axis runs over, the one named last changes fastest.
Arguments:
- queries: bfloat16 [16, 64, 4, 1536], P('tm', 'height'), may hold values from -6 to 6
- key_tokens: bfloat16 [16, 64, 4, 1536], P('tm', 'height'), may hold values from -6 to 6
- value_tokens: bfloat16 [16, 64, 4, 1536], P('tm', 'height'), may hold values from -6 to 6
- out_weight: bfloat16 [1536, 3072], P('height'), may hold values from -0.15625 to 0.15625
- out_grad: bfloat16 [16, 64, 4, 3072], P('tm', 'height'), may hold values from -6 to 6
- window_reach: int32 [4, 8, 2], replicated, may hold values from 0 to 2, as said below
- tile_valid: int32 [4, 8], replicated, may hold values 0 or 1
Outputs:
- attn_out: bfloat16 [16, 64, 4, 3072], P('tm', 'height')
- grad_query: bfloat16 [16, 64, 4, 1536], P('tm', 'height')
- grad_key: bfloat16 [16, 64, 4, 1536], P('tm', 'height')
- grad_value: bfloat16 [16, 64, 4, 1536], P('tm', 'height')
- grad_weight: float32 [1536, 3072], P('height', 'tm')
Inputs may be any that keep to these rules, and one draw needn't show every extreme that they name: `window_reach`: entry 0 is a tile's reach in frames and entry 1 its reach in rows; some tile reaches 2 in both.
All inputs are finite; a program needn't handle non-finite values.
Results may differ from a plain program's by a relative error of at most 0.014.
Values may be sent and summed in bfloat16 or wider, within the bound.
A program may use at most 128 MiB of HBM per device.

v0:
```python
import math
import jax
import jax.numpy as jnp
from jax import lax
from jax.sharding import PartitionSpec as P

HEAD_DIM = 128
HALO = 2


def padded(shard, sides, width):
    for axis, dim in sides:
        count, length = (lax.axis_size(axis), shard.shape[dim])
        up = [(i, (i + 1) % count) for i in range(count - 1)]
        down = [(j, i) for i, j in up]
        last = lax.slice_in_dim(shard, length - width, length, axis=dim)
        first = lax.slice_in_dim(shard, 0, width, axis=dim)
        before = lax.ppermute(last, axis, up)
        after = lax.ppermute(first, axis, down)
        shard = jnp.concatenate([before, shard, after], axis=dim)
    return shard


def passed_along(value, axis, steps):
    count = lax.axis_size(axis)
    first, last = (max(0, -steps), min(count, count - steps))
    return lax.ppermute(value, axis, [(source, source + steps) for source in range(first, last)])


def key_mask(
    window_reach, tile_valid, frame_tile, row_tile, tile_frames, tile_rows, margin, columns
):
    tiles_frames = tile_valid.shape[0]
    tiles_rows = tile_valid.shape[1]
    ext_frames = tile_frames + 2 * margin
    ext_rows = tile_rows + 2 * margin
    frame_pos = jnp.arange(ext_frames, dtype=jnp.int32)
    row_pos = jnp.arange(ext_rows, dtype=jnp.int32)
    frame_ids = jnp.arange(tiles_frames, dtype=jnp.int32)
    row_ids = jnp.arange(tiles_rows, dtype=jnp.int32)
    marked = (frame_ids[:, None] == frame_tile) & (row_ids[None, :] == row_tile)
    reach_frame = jnp.sum(jnp.where(marked, window_reach[:, :, 0], 0))
    reach_row = jnp.sum(jnp.where(marked, window_reach[:, :, 1], 0))
    global_frame = frame_tile * tile_frames - margin + frame_pos
    global_row = row_tile * tile_rows - margin + row_pos
    own_frame = (frame_pos >= margin) & (frame_pos < margin + tile_frames)
    own_row = (row_pos >= margin) & (row_pos < margin + tile_rows)
    near_frame = (frame_pos >= margin - reach_frame) & (
        frame_pos < margin + tile_frames + reach_frame
    )
    near_frame = near_frame & (global_frame >= 0) & (global_frame < tiles_frames * tile_frames)
    near_row = (row_pos >= margin - reach_row) & (row_pos < margin + tile_rows + reach_row)
    near_row = near_row & (global_row >= 0) & (global_row < tiles_rows * tile_rows)
    onehot_frame = (
        jnp.floor_divide(global_frame, tile_frames)[:, None] == frame_ids[None, :]
    ).astype(jnp.float32)
    onehot_row = (jnp.floor_divide(global_row, tile_rows)[:, None] == row_ids[None, :]).astype(
        jnp.float32
    )
    valid = jnp.dot(jnp.dot(onehot_frame, tile_valid.astype(jnp.float32)), onehot_row.T) > 0.5
    allowed = (
        own_frame[:, None] & own_row[None, :] | near_frame[:, None] & near_row[None, :] & valid
    )
    return jnp.broadcast_to(allowed[:, :, None], (ext_frames, ext_rows, columns)).reshape(-1)


def attend(tile_queries, ext_keys, ext_values, d_mixed, allowed):
    score_scale = 1.0 / math.sqrt(HEAD_DIM)
    scores = (
        jnp.einsum("qhd,khd->hqk", tile_queries, ext_keys, preferred_element_type=jnp.float32)
        * score_scale
    )
    scores = jnp.where(allowed[None, None, :], scores, -1e30)
    row_max = jnp.max(scores, axis=-1, keepdims=True)
    expo = jnp.exp(scores - row_max)
    prob = expo / jnp.sum(expo, axis=-1, keepdims=True)
    probs = prob.astype(jnp.bfloat16)
    mixed = jnp.einsum(
        "hqk,khd->qhd", probs, ext_values, preferred_element_type=jnp.float32
    ).astype(jnp.bfloat16)
    d_probs = jnp.einsum("qhd,khd->hqk", d_mixed, ext_values, preferred_element_type=jnp.float32)
    inner = jnp.sum(prob * d_probs, axis=-1, keepdims=True)
    d_scores = (prob * (d_probs - inner) * score_scale).astype(jnp.bfloat16)
    d_query = jnp.einsum(
        "hqk,khd->qhd", d_scores, ext_keys, preferred_element_type=jnp.float32
    ).astype(jnp.bfloat16)
    d_key = jnp.einsum("hqk,qhd->khd", d_scores, tile_queries, preferred_element_type=jnp.float32)
    d_value = jnp.einsum("hqk,qhd->khd", probs, d_mixed, preferred_element_type=jnp.float32)
    return (mixed, d_query, d_key, d_value)


def shards(queries, key_tokens, value_tokens, out_weight, out_grad, window_reach, tile_valid):
    tile_frames, tile_rows, columns, width = queries.shape
    model_width = out_grad.shape[3]
    tokens = tile_frames * tile_rows * columns
    heads = width // HEAD_DIM
    margin = HALO
    ext_frames = tile_frames + 2 * margin
    ext_rows = tile_rows + 2 * margin
    ext_count = ext_frames * ext_rows * columns
    full_weight = lax.all_gather(out_weight, "height", axis=0, tiled=True)
    grad_rows = out_grad.reshape(tokens, model_width)
    d_mixed = lax.dot_general(
        grad_rows, full_weight, (((1,), (1,)), ((), ())), preferred_element_type=jnp.float32
    ).astype(jnp.bfloat16)
    stacked = jnp.stack([key_tokens, value_tokens], axis=3)
    extended = padded(stacked, (("tm", 0), ("height", 1)), margin)
    ext_keys = extended[:, :, :, 0, :].reshape(ext_count, heads, HEAD_DIM)
    ext_values = extended[:, :, :, 1, :].reshape(ext_count, heads, HEAD_DIM)
    frame_tile = lax.axis_index("tm")
    row_tile = lax.axis_index("height")
    allowed = key_mask(
        window_reach, tile_valid, frame_tile, row_tile, tile_frames, tile_rows, margin, columns
    )
    mixed, d_query, d_key, d_value = attend(
        queries.reshape(tokens, heads, HEAD_DIM),
        ext_keys,
        ext_values,
        d_mixed.reshape(tokens, heads, HEAD_DIM),
        allowed,
    )
    mixed_rows = mixed.reshape(tokens, width)
    attn_out = jnp.dot(mixed_rows, full_weight, preferred_element_type=jnp.float32).astype(
        jnp.bfloat16
    )
    attn_out = attn_out.reshape(tile_frames, tile_rows, columns, model_width)
    row_share = lax.psum_scatter(
        lax.dot_general(
            mixed_rows, grad_rows, (((0,), (0,)), ((), ())), preferred_element_type=jnp.float32
        ).astype(jnp.bfloat16),
        "height",
        scatter_dimension=0,
        tiled=True,
    )
    grad_weight = lax.psum_scatter(row_share, "tm", scatter_dimension=1, tiled=True).astype(
        jnp.float32
    )
    key_value_grads = jnp.stack(
        [d_key.reshape(ext_count, width), d_value.reshape(ext_count, width)], axis=1
    )
    key_value_grads = key_value_grads.reshape(ext_frames, ext_rows, columns, 2, width)
    upper_rows = key_value_grads[:, :margin]
    lower_rows = key_value_grads[:, margin + tile_rows :]
    middle_rows = key_value_grads[:, margin : margin + tile_rows]
    from_next_row = passed_along(upper_rows.astype(jnp.bfloat16), "height", -1).astype(
        upper_rows.dtype
    )
    from_prev_row = passed_along(lower_rows.astype(jnp.bfloat16), "height", 1).astype(
        lower_rows.dtype
    )
    middle_rows = jnp.concatenate(
        [
            middle_rows[:, :margin] + from_prev_row,
            middle_rows[:, margin : tile_rows - margin],
            middle_rows[:, tile_rows - margin :] + from_next_row,
        ],
        axis=1,
    )
    upper_frames = middle_rows[:margin]
    lower_frames = middle_rows[margin + tile_frames :]
    middle_frames = middle_rows[margin : margin + tile_frames]
    from_next_frame = passed_along(upper_frames.astype(jnp.bfloat16), "tm", -1).astype(
        upper_frames.dtype
    )
    from_prev_frame = passed_along(lower_frames.astype(jnp.bfloat16), "tm", 1).astype(
        lower_frames.dtype
    )
    own_grads = jnp.concatenate(
        [
            middle_frames[:margin] + from_prev_frame,
            middle_frames[margin : tile_frames - margin],
            middle_frames[tile_frames - margin :] + from_next_frame,
        ],
        axis=0,
    )
    grad_query = d_query.reshape(tile_frames, tile_rows, columns, width)
    grad_key = own_grads[:, :, :, 0, :].astype(jnp.bfloat16)
    grad_value = own_grads[:, :, :, 1, :].astype(jnp.bfloat16)
    return (attn_out, grad_query, grad_key, grad_value, grad_weight)


def solution(mesh):
    return jax.shard_map(
        shards,
        mesh=mesh,
        in_specs=(
            P("tm", "height", None, None),
            P("tm", "height", None, None),
            P("tm", "height", None, None),
            P("height", None),
            P("tm", "height", None, None),
            P(),
            P(),
        ),
        out_specs=(
            P("tm", "height", None, None),
            P("tm", "height", None, None),
            P("tm", "height", None, None),
            P("tm", "height", None, None),
            P("height", "tm"),
        ),
        check_vma=False,
    )
```

profile of v0, /device:TPU:0, one launch (start us, length us, event | category | flops | bytes accessed | tf_op | source)
XLA Modules:
  0.0 367.9 jit_solution(9377724077778961661)
XLA Ops:
  7.3 0.7 all-gather.2.cloned.1.call-update
  7.9 0.0 reduce-scatter.3.cloned.1.call-start
  8.0 1.9 fusion.46
  9.9 1.3 collective-permute-start.1
  11.2 3.1 collective-permute-start
  14.3 1.1 reshape.126
  15.3 0.7 fusion.51
  18.7 1.5 pad_maximum_fusion.5
  20.2 1.3 collective-permute-start.3
  21.5 6.3 %collective-permute-start.2 = (bf16[8,2,4,2,1536]{4,2,1,0,3:T(4,128)(2,1)}, bf16[8,2,4,2,1536]{4,2,1,0,3:T(4,128)(2,1)}, u32[]{:S(2)}, u32[]{:S(2)}) collective-permute-start(bf16[8,2,4,2,1536]{4,2,1,0,3:T(4,128)(2,1)} %get-tuple-element.22), channel_id=1, source_target_pairs={{0,1},{1,2},{2,3},{3,4},{4,5},{5,6},{6,7},{8,9},{9,10},{10,11},{11... | collective-permute-start | bytes 1179656 | tf_op jit(solution)/shard_map/ppermute | solution.py:18
  27.8 1.0 fusion.38
  28.8 0.1 broadcast_in_dim.18
  28.9 0.1 broadcast_in_dim.19
  29.0 0.2 reshape.129
  29.2 14.2 %collective-permute-done.3 = bf16[8,2,4,2,1536]{4,2,1,0,3:T(4,128)(2,1)S(1)} collective-permute-done((bf16[8,2,4,2,1536]{4,2,1,0,3:T(4,128)(2,1)}, bf16[8,2,4,2,1536]{4,2,1,0,3:T(4,128)(2,1)S(1)}, u32[]{:S(2)}, u32[]{:S(2)}) %collective-permute-start.3) | collective-permute-done | bytes 393248 | tf_op jit(solution)/shard_map/ppermute | solution.py:19
  43.4 6.6 %collective-permute-done.2 = bf16[8,2,4,2,1536]{4,2,1,0,3:T(4,128)(2,1)} collective-permute-done((bf16[8,2,4,2,1536]{4,2,1,0,3:T(4,128)(2,1)}, bf16[8,2,4,2,1536]{4,2,1,0,3:T(4,128)(2,1)}, u32[]{:S(2)}, u32[]{:S(2)}) %collective-permute-start.2) | collective-permute-done | bytes 393248 | tf_op jit(solution)/shard_map/ppermute | solution.py:18
  50.0 3.2 pad_maximum_fusion.1
  53.1 0.9 fusion.65
  54.0 1.7 reshape_squeeze.6
  55.7 0.8 reshape_squeeze.7
  56.5 1.3 copy.35
  57.8 1.9 fusion.48
  59.8 0.8 fusion.68
  60.7 0.6 copy-done
  61.2 0.8 convolution_convert_fusion.3
  62.0 0.1 copy-done.9
  62.1 5.0 %convolution_convert_fusion = bf16[1536,3072]{1,0:T(8,128)(2,1)} fusion(bf16[128,1536]{0,1:T(8,128)(2,1)S(1)} %bitcast.51, bf16[128,3072]{1,0:T(8,128)(2,1)S(1)} %reshape.129), kind=kOutput, calls=%fused_computation.2 | convolution fusion | flops 1212678144 | bytes 10616832 | tf_op jit(solution)/shard_map/dot_general | solution.py:128
  67.1 0.2 reduce-scatter.5.cloned.1.call-start
  67.3 91.7 %all-gather.2.cloned.1.call-done = bf16[1536,3072]{1,0:T(8,128)(2,1)} async-done(((bf16[192,3072]{1,0:T(8,128)(2,1)}), bf16[1536,3072]{1,0:T(8,128)(2,1)}) %all-gather.2.cloned.1.call-update) | async-done | bytes 9437200 | tf_op jit(solution)/shard_map/all_gather | solution.py:101
  159.0 6.9 %convolution_convert_fusion.2 = bf16[128,1536]{1,0:T(8,128)(2,1)S(1)} fusion(bf16[128,3072]{1,0:T(8,128)(2,1)S(1)} %reshape.129, bf16[1536,3072]{1,0:T(8,128)(2,1)} %all-gather.2.cloned.1.call-done), kind=kOutput, calls=%fused_computation.5 | convolution fusion | flops 1208156160 | bytes 10616832 | tf_op jit(solution)/shard_map/dot_general | solution.py:103
  165.9 0.2 copy.30
  166.2 1.9 fusion.42
  168.1 6.3 %fusion.15 = f32[384,12,128]{2,0,1:T(8,128)} fusion(f32[12,128,384]{1,2,0:T(8,128)} %fusion.42, bf16[128,12,128]{2,1,0:T(8,128)(2,1)S(1)} %copy-done.4, f32[12,128,384]{1,2,0:T(8,128)} %copy-done.9, f32[12,128]{1,0:T(8,128)S(1)} %get-tuple-element.30), kind=kOutput, calls=%fused_computation.18 | convolution fusion | flops 155125632 | bytes 7477248 | tf_op jit(solution)/shard_map/hqk,qhd->khd/dot_general | solution.py:87
  174.4 3.1 copy.39
  177.5 2.0 stack.19
  179.4 3.8 %convolution_bitcast_fusion = f32[384,12,128]{0,2,1:T(8,128)} fusion(bf16[128,12,128]{0,2,1:T(8,128)(2,1)} %bitcast.54, f32[12,128,384]{1,2,0:T(8,128)} %copy-done.9, f32[12,128]{1,0:T(8,128)S(1)} %get-tuple-element.30), kind=kOutput, calls=%fused_computation.17 | convolution fusion | flops 152174592 | bytes 5117952 | tf_op jit(solution)/shard_map/hqk,qhd->khd/dot_general | solution.py:88
  183.2 2.6 copy.41
  185.9 1.9 stack.20
  187.8 2.1 constant_dynamic-update-slice_fusion.1
  189.9 2.1 constant_dynamic-update-slice_fusion
  192.1 1.0 convert.12
  193.0 0.1 slice.95
  193.2 0.3 fusion.64
  193.5 3.1 collective-permute-start.4
  196.6 1.3 collective-permute-start.5
  198.0 2.3 convolution_convert_fusion.1
  200.3 13.5 %collective-permute-done.4 = bf16[8,2,4,2,1536]{4,2,1,0,3:T(4,128)(2,1)S(1)} collective-permute-done((bf16[8,2,4,2,1536]{4,2,1,0,3:T(4,128)(2,1)S(1)}, bf16[8,2,4,2,1536]{4,2,1,0,3:T(4,128)(2,1)S(1)}, u32[]{:S(2)}, u32[]{:S(2)}) %collective-permute-start.4) | collective-permute-done | bytes 393248 | tf_op jit(solution)/shard_map/ppermute | solution.py:27
  213.8 2.4 collective-permute-done.5
  216.2 0.5 slice_add_fusion.3
  216.7 115.4 %reduce-scatter.3.cloned.1.call-done = bf16[192,3072]{1,0:T(8,128)(2,1)} async-done(((bf16[1536,3072]{1,0:T(8,128)(2,1)}), bf16[192,3072]{1,0:T(8,128)(2,1)}) %reduce-scatter.3.cloned.1.call-update) | async-done | bytes 1179664 | tf_op jit(solution)/shard_map/reduce_scatter | solution.py:127
  332.1 1.0 fusion.63
  333.1 1.2 fusion.66
  334.3 1.8 collective-permute-start.6
  336.1 1.5 collective-permute-start.7
  337.6 6.4 %fusion.21 = bf16[128,12,128]{0,2,1:T(8,128)(2,1)} fusion(bf16[384,12,128]{0,2,1:T(8,128)(2,1)} %copy-done.1, f32[12,128,384]{1,2,0:T(8,128)} %fusion.42, f32[12,128,384]{1,2,0:T(8,128)} %copy-done.9, f32[12,128]{1,0:T(8,128)S(1)} %get-tuple-element.30), kind=kOutput, calls=%fused_computation.22 | convolution fusion | flops 155322240 | bytes 6297600 | tf_op jit(solution)/shard_map/hqk,khd->qhd/dot_general | solution.py:84
  344.0 2.4 reshape.128
  346.4 2.2 copy.37
  348.5 2.0 reshape.131
  350.5 0.8 pad_maximum_fusion
  351.3 1.5 slice_add_fusion.1
  352.8 0.5 maximum_convert_fusion
  353.3 1.2 slice_bitcast_fusion
  354.5 5.0 %reduce-scatter.5.cloned.1.call-done = bf16[192,768]{1,0:T(8,128)(2,1)} async-done(((bf16[192,3072]{1,0:T(8,128)(2,1)}), bf16[192,768]{1,0:T(8,128)(2,1)}) %reduce-scatter.5.cloned.1.call-update) | async-done | bytes 294928 | tf_op jit(solution)/shard_map/reduce_scatter | solution.py:135
  359.5 1.8 convert_element_type.75
  (39 shorter events, 0.2 us)
Async XLA Ops:
  7.2 11.5 %copy-start.2 = (bf16[4,8,4,1536]{3,2,1,0:T(4,128)(2,1)S(1)}, bf16[4,8,4,1536]{3,2,1,0:T(4,128)(2,1)}, u32[]{:S(2)}) copy-start(bf16[4,8,4,1536]{3,2,1,0:T(4,128)(2,1)} %param.8) | copy-start | bytes 1179652
  7.2 11.5 %copy-start.3 = (bf16[4,8,4,1536]{3,2,1,0:T(4,128)(2,1)S(1)}, bf16[4,8,4,1536]{3,2,1,0:T(4,128)(2,1)}, u32[]{:S(2)}) copy-start(bf16[4,8,4,1536]{3,2,1,0:T(4,128)(2,1)} %param.9) | copy-start | bytes 1179652
  7.2 7.1 %copy-start.8 = (s32[4,8,2]{1,2,0:T(2,128)S(1)}, s32[4,8,2]{1,2,0:T(2,128)}, u32[]{:S(2)}) copy-start(s32[4,8,2]{1,2,0:T(2,128)} %param.12) | copy-start | bytes 772
  7.2 7.1 %copy-start.7 = (bf16[4,8,4,1536]{3,2,1,0:T(4,128)(2,1)S(1)}, bf16[4,8,4,1536]{3,2,1,0:T(4,128)(2,1)}, u32[]{:S(2)}) copy-start(bf16[4,8,4,1536]{3,2,1,0:T(4,128)(2,1)} %param.7) | copy-start | bytes 1179652
  7.2 151.8 %all-gather.2.cloned.1.call-start = ((), (), s32[]{:S(2)}) async-start(), calls=%async_computation.2 | async-start | bytes 10616832 | tf_op jit(solution)/shard_map/all_gather | solution.py:101
  7.9 324.2 %reduce-scatter.3.cloned.1.call-start = ((), (), s32[]{:S(2)}) async-start(), calls=%async_computation.3 | async-start | bytes 10616832 | tf_op jit(solution)/shard_map/reduce_scatter | solution.py:127
  8.0 21.0 %copy-start.6 = (bf16[4,8,4,3072]{3,2,1,0:T(4,128)(2,1)S(1)}, bf16[4,8,4,3072]{3,2,1,0:T(4,128)(2,1)}, u32[]{:S(2)}) copy-start(bf16[4,8,4,3072]{3,2,1,0:T(4,128)(2,1)} %param.11) | copy-start | bytes 2359300
  9.9 8.8 %collective-permute-start.1 = (bf16[2,8,4,2,1536]{4,2,1,0,3:T(4,128)(2,1)S(1)}, bf16[2,8,4,2,1536]{4,2,1,0,3:T(4,128)(2,1)S(1)}, u32[]{:S(2)}, u32[]{:S(2)}) collective-permute-start(bf16[2,8,4,2,1536]{4,2,1,0,3:T(4,128)(2,1)S(1)} %get-tuple-element.27), channel_id=1, source_target_pairs={{8,0},{16,8},{24,16},{9,1},{17,9},{25,17},{10,2},{18,10},{26,18},{... | collective-permute-start | bytes 1179656 | tf_op jit(solution)/shard_map/ppermute | solution.py:19
  11.2 7.5 %collective-permute-start = (bf16[2,8,4,2,1536]{4,2,1,0,3:T(4,128)(2,1)S(1)}, bf16[2,8,4,2,1536]{4,2,1,0,3:T(4,128)(2,1)S(1)}, u32[]{:S(2)}, u32[]{:S(2)}) collective-permute-start(bf16[2,8,4,2,1536]{4,2,1,0,3:T(4,128)(2,1)S(1)} %get-tuple-element.26), channel_id=1, source_target_pairs={{0,8},{8,16},{16,24},{1,9},{9,17},{17,25},{2,10},{10,18},{18,26},{... | collective-permute-start | bytes 1179656 | tf_op jit(solution)/shard_map/ppermute | solution.py:18
  20.2 23.2 %collective-permute-start.3 = (bf16[8,2,4,2,1536]{4,2,1,0,3:T(4,128)(2,1)}, bf16[8,2,4,2,1536]{4,2,1,0,3:T(4,128)(2,1)S(1)}, u32[]{:S(2)}, u32[]{:S(2)}) collective-permute-start(bf16[8,2,4,2,1536]{4,2,1,0,3:T(4,128)(2,1)} %get-tuple-element.23), channel_id=1, source_target_pairs={{1,0},{2,1},{3,2},{4,3},{5,4},{6,5},{7,6},{9,8},{10,9},{11,10},{12... | collective-permute-start | bytes 1179656 | tf_op jit(solution)/shard_map/ppermute | solution.py:19
  21.5 28.5 %collective-permute-start.2 = (bf16[8,2,4,2,1536]{4,2,1,0,3:T(4,128)(2,1)}, bf16[8,2,4,2,1536]{4,2,1,0,3:T(4,128)(2,1)}, u32[]{:S(2)}, u32[]{:S(2)}) collective-permute-start(bf16[8,2,4,2,1536]{4,2,1,0,3:T(4,128)(2,1)} %get-tuple-element.22), channel_id=1, source_target_pairs={{0,1},{1,2},{2,3},{3,4},{4,5},{5,6},{6,7},{8,9},{9,10},{10,11},{11... | collective-permute-start | bytes 1179656 | tf_op jit(solution)/shard_map/ppermute | solution.py:18
  57.8 2.8 copy-start.1
  59.8 1.4 copy-start
  60.7 1.4 copy-start.9
  67.1 292.4 %reduce-scatter.5.cloned.1.call-start = ((), (), s32[]{:S(2)}) async-start(), calls=%async_computation.4 | async-start | bytes 1474560 | tf_op jit(solution)/shard_map/reduce_scatter | solution.py:135
  165.9 2.2 copy-start.4
  166.2 1.9 copy-start.5
  187.8 10.2 %slice-start = ((s8[9437184]{0:T(1024)(128)(4,1)}), s8[4194304]{0:T(1024)(128)(4,1)S(1)}, s32[]{:S(2)}) async-start(s8[9437184]{0:T(1024)(128)(4,1)} %bitcast.43), calls=%async_computation.5 | async-start | bytes 8388608
  189.9 8.0 %slice-start.1 = ((s8[9437184]{0:T(1024)(128)(4,1)}), s8[4194304]{0:T(1024)(128)(4,1)S(1)}, s32[]{:S(2)}) async-start(s8[9437184]{0:T(1024)(128)(4,1)} %bitcast.43), calls=%async_computation.6 | async-start | bytes 8388608
  192.0 5.9 %slice-start.2 = ((s8[9437184]{0:T(1024)(128)(4,1)}), s8[1048576]{0:T(1024)(128)(4,1)S(1)}, s32[]{:S(2)}) async-start(s8[9437184]{0:T(1024)(128)(4,1)} %bitcast.43), calls=%async_computation.7 | async-start | bytes 2097152
  193.5 20.3 %collective-permute-start.4 = (bf16[8,2,4,2,1536]{4,2,1,0,3:T(4,128)(2,1)S(1)}, bf16[8,2,4,2,1536]{4,2,1,0,3:T(4,128)(2,1)S(1)}, u32[]{:S(2)}, u32[]{:S(2)}) collective-permute-start(bf16[8,2,4,2,1536]{4,2,1,0,3:T(4,128)(2,1)S(1)} %get-tuple-element.16), channel_id=1, source_target_pairs={{0,1},{1,2},{2,3},{3,4},{4,5},{5,6},{6,7},{8,9},{9,10},{10,11},{11... | collective-permute-start | bytes 1179656 | tf_op jit(solution)/shard_map/ppermute | solution.py:27
  196.6 19.6 %collective-permute-start.5 = (bf16[8,2,4,2,1536]{4,2,1,0,3:T(4,128)(2,1)S(1)}, bf16[8,2,4,2,1536]{4,2,1,0,3:T(4,128)(2,1)S(1)}, u32[]{:S(2)}, u32[]{:S(2)}) collective-permute-start(bf16[8,2,4,2,1536]{4,2,1,0,3:T(4,128)(2,1)S(1)} %get-tuple-element.17), channel_id=1, source_target_pairs={{1,0},{2,1},{3,2},{4,3},{5,4},{6,5},{7,6},{9,8},{10,9},{11,10},{12... | collective-permute-start | bytes 1179656 | tf_op jit(solution)/shard_map/ppermute | solution.py:27
  334.3 17.0 %collective-permute-start.6 = (bf16[2,8,4,2,1536]{4,2,1,0,3:T(4,128)(2,1)}, bf16[2,8,4,2,1536]{4,2,1,0,3:T(4,128)(2,1)S(1)}, u32[]{:S(2)}, u32[]{:S(2)}) collective-permute-start(bf16[2,8,4,2,1536]{4,2,1,0,3:T(4,128)(2,1)} %get-tuple-element.20), channel_id=1, source_target_pairs={{0,8},{8,16},{16,24},{1,9},{9,17},{17,25},{2,10},{10,18},{18,26},{... | collective-permute-start | bytes 1179656 | tf_op jit(solution)/shard_map/ppermute | solution.py:27
  336.1 15.2 %collective-permute-start.7 = (bf16[2,8,4,2,1536]{4,2,1,0,3:T(4,128)(2,1)}, bf16[2,8,4,2,1536]{4,2,1,0,3:T(4,128)(2,1)}, u32[]{:S(2)}, u32[]{:S(2)}) collective-permute-start(bf16[2,8,4,2,1536]{4,2,1,0,3:T(4,128)(2,1)} %get-tuple-element.21), channel_id=1, source_target_pairs={{8,0},{16,8},{24,16},{9,1},{17,9},{25,17},{10,2},{18,10},{26,18},{... | collective-permute-start | bytes 1179656 | tf_op jit(solution)/shard_map/ppermute | solution.py:27
Sparse Core Ops, SparseCore 0:
  10.2 148.7 all-gather.1
  162.6 169.4 reduce-scatter.2
  334.7 24.8 reduce-scatter.4
where the time goes:
time: 369 us; the launch traced here: 368 us
  waiting for transfers between devices  250 us (68%)
  matrix products  36.3 us (10%)
  local copies, waits for them, and re-layouts  30.1 us (8%)
  starting transfers between devices  19.9 us (5%)
  between operations  16.8 us (5%)
  other arithmetic  15.2 us (4%)
    reduce_scatter x1, waiting for transfers between devices, shards(): lax.psum_scatter(lax.dot_general(mixed_rows, grad_rows, (((0,), (0,)), ((...  115 us
    all_gather x1, waiting for transfers between devices, shards(): full_weight = lax.all_gather(out_weight, 'height', axis=0, tiled=True)  91.7 us
    ppermute x4, waiting for transfers between devices, passed_along(): lax.ppermute(value, axis, [(source, source + steps) for source in range(f...  15.9 us
    ppermute x2, waiting for transfers between devices, padded(): after = lax.ppermute(first, axis, down)  14.2 us
    ppermute x2, starting transfers between devices, padded(): before = lax.ppermute(last, axis, up)  9.32 us
    ppermute x4, starting transfers between devices, passed_along(): lax.ppermute(value, axis, [(source, source + steps) for source in range(f...  7.74 us
  transfers between devices with their start and end apart: 11, of which 7 were waited for; matrix products, arithmetic and copies ran while one was open for 21% of the time, Pallas kernels for 0%

commit v1 on v0

--- a/solution.py
+++ b/solution.py
@@ -98,7 +98,14 @@
     ext_frames = tile_frames + 2 * margin
     ext_rows = tile_rows + 2 * margin
     ext_count = ext_frames * ext_rows * columns
-    full_weight = lax.all_gather(out_weight, "height", axis=0, tiled=True)
+    ring = [out_weight]
+    for hop in range(7):
+        ring.append(lax.ppermute(ring[-1], "height", [(dev, (dev + 1) % 8) for dev in range(8)]))
+    full_weight = jnp.roll(
+        jnp.concatenate(ring[::-1], axis=0),
+        (lax.axis_index("height") + 1) * ring[0].shape[0],
+        axis=0,
+    )
     grad_rows = out_grad.reshape(tokens, model_width)
     d_mixed = lax.dot_general(
         grad_rows, full_weight, (((1,), (1,)), ((), ())), preferred_element_type=jnp.float32

time: 369 us -> 448 us (1.21)
  waiting for transfers between devices: 250 us -> 303 us
  local copies, waits for them, and re-layouts: 30.1 us -> 53.5 us
    ppermute x0 -> x7, waiting for transfers between devices: none -> 274 us  [shards(): lax.ppermute(ring[-1], 'height', [(dev, (dev + 1) % 8) for dev in range(8)])]
    reduce_scatter x1, waiting for transfers between devices: 115 us -> 9.47 us  [shards(): lax.psum_scatter(lax.dot_general(mixed_rows, grad_rows, (((0,), (0,)), ((...]
    all_gather x1 -> x0, waiting for transfers between devices: 91.7 us -> none  [shards(): full_weight = lax.all_gather(out_weight, 'height', axis=0, tiled=True)]
    unnamed x27 -> x62, local copies, waits for them, and re-layouts: 2.8 us -> 22.3 us
    ppermute x4, waiting for transfers between devices: 15.9 us -> 0.41 us  [passed_along(): lax.ppermute(value, axis, [(source, source + steps) for source in range(f...]
    ppermute x2, waiting for transfers between devices: 14.2 us -> 0.01 us  [padded(): after = lax.ppermute(first, axis, down)]
    ppermute x0 -> x7, starting transfers between devices: none -> 8.34 us  [shards(): lax.ppermute(ring[-1], 'height', [(dev, (dev + 1) % 8) for dev in range(8)])]
    dot_general x1, matrix products: 2.33 us -> 7.6 us  [shards(): jnp.dot(mixed_rows, full_weight, preferred_element_type=jnp.float32)]
  transfers between devices with their start and end apart: 11 -> 17, of which waited for: 7 -> 11; matrix products, arithmetic and copies ran while one was open for 21% -> 15% of each run, Pallas kernels for 0% -> 0%
where the time goes in v1:
time: 448 us; the launch traced here: 447 us
  waiting for transfers between devices  303 us (68%)
  local copies, waits for them, and re-layouts  53.5 us (12%)
  matrix products  34.2 us (8%)
  starting transfers between devices  23.2 us (5%)
  between operations  17.2 us (4%)
  other arithmetic  16.1 us (4%)
    ppermute x7, waiting for transfers between devices, shards(): lax.ppermute(ring[-1], 'height', [(dev, (dev + 1) % 8) for dev in range(8)])  274 us
    unnamed x62, local copies, waits for them, and re-layouts  22.3 us
    ppermute x2, waiting for transfers between devices, padded(): before = lax.ppermute(last, axis, up)  10.1 us
    reduce_scatter x1, waiting for transfers between devices, shards(): lax.psum_scatter(lax.dot_general(mixed_rows, grad_rows, (((0,), (0,)), ((...  9.47 us
  transfers between devices with their start and end apart: 17, of which 11 were waited for; matrix products, arithmetic and copies ran while one was open for 15% of the time, Pallas kernels for 0%

profile of v1, /device:TPU:0, one launch (start us, length us, event | category | flops | bytes accessed | tf_op | source)
XLA Modules:
  0.0 446.8 jit_solution(12593749229126414763)
XLA Ops:
  7.2 1.9 fusion.56
  9.1 2.5 collective-permute-start
  11.6 1.3 collective-permute-start.1
  13.7 1.6 reshape.129
  19.2 1.4 pad_maximum_fusion.5
  20.6 4.3 collective-permute-start.2
  24.9 1.3 collective-permute-start.3
  26.7 1.6 fusion.48
  29.6 1.1 reshape.126
  30.7 10.0 %collective-permute-done.2 = bf16[8,2,4,2,1536]{4,2,1,0,3:T(4,128)(2,1)S(1)} collective-permute-done((bf16[8,2,4,2,1536]{4,2,1,0,3:T(4,128)(2,1)}, bf16[8,2,4,2,1536]{4,2,1,0,3:T(4,128)(2,1)S(1)}, u32[]{:S(2)}, u32[]{:S(2)}) %collective-permute-start.2) | collective-permute-done | bytes 393248 | tf_op jit(solution)/shard_map/ppermute | solution.py:18
  40.8 3.2 pad_maximum_fusion.1
  43.9 2.1 fusion.77
  46.8 1.3 copy.33
  48.1 3.1 reshape_squeeze.6
  51.2 2.0 fusion.58
  55.6 5.0 %convolution_convert_fusion = bf16[1536,3072]{1,0:T(8,128)(2,1)} fusion(bf16[128,1536]{0,1:T(8,128)(2,1)S(1)} %bitcast.49, bf16[128,3072]{1,0:T(8,128)(2,1)S(1)} %reshape.129), kind=kOutput, calls=%fused_computation.2 | convolution fusion | flops 1212678144 | bytes 10616832 | tf_op jit(solution)/shard_map/dot_general | solution.py:135
  60.7 1.2 copy-done.3
  61.9 2.4 collective-permute-start.4
  64.3 48.3 %collective-permute-done.4 = bf16[192,3072]{1,0:T(8,128)(2,1)S(1)} collective-permute-done((bf16[192,3072]{1,0:T(8,128)(2,1)S(1)}, bf16[192,3072]{1,0:T(8,128)(2,1)S(1)}, u32[]{:S(2)}, u32[]{:S(2)}) %collective-permute-start.4) | collective-permute-done | bytes 1179680 | tf_op jit(solution)/shard_map/ppermute | solution.py:103
  112.5 2.9 collective-permute-start.5
  115.4 53.5 %collective-permute-done.5 = bf16[192,3072]{1,0:T(8,128)(2,1)S(1)} collective-permute-done((bf16[192,3072]{1,0:T(8,128)(2,1)S(1)}, bf16[192,3072]{1,0:T(8,128)(2,1)S(1)}, u32[]{:S(2)}, u32[]{:S(2)}) %collective-permute-start.5) | collective-permute-done | bytes 1179680 | tf_op jit(solution)/shard_map/ppermute | solution.py:103
  169.5 52.1 %collective-permute-done.6 = bf16[192,3072]{1,0:T(8,128)(2,1)S(1)} collective-permute-done((bf16[192,3072]{1,0:T(8,128)(2,1)S(1)}, bf16[192,3072]{1,0:T(8,128)(2,1)S(1)}, u32[]{:S(2)}, u32[]{:S(2)}) %collective-permute-start.6) | collective-permute-done | bytes 1179680 | tf_op jit(solution)/shard_map/ppermute | solution.py:103
  221.6 1.0 copy-done.4
  222.6 37.5 %collective-permute-done.7 = bf16[192,3072]{1,0:T(8,128)(2,1)S(1)} collective-permute-done((bf16[192,3072]{1,0:T(8,128)(2,1)S(1)}, bf16[192,3072]{1,0:T(8,128)(2,1)S(1)}, u32[]{:S(2)}, u32[]{:S(2)}) %collective-permute-start.7) | collective-permute-done | bytes 1179680 | tf_op jit(solution)/shard_map/ppermute | solution.py:103
  260.1 1.0 copy-done.6
  261.1 2.5 collective-permute-start.8
  263.6 26.7 %collective-permute-done.8 = bf16[192,3072]{1,0:T(8,128)(2,1)S(1)} collective-permute-done((bf16[192,3072]{1,0:T(8,128)(2,1)S(1)}, bf16[192,3072]{1,0:T(8,128)(2,1)S(1)}, u32[]{:S(2)}, u32[]{:S(2)}) %collective-permute-start.8) | collective-permute-done | bytes 1179680 | tf_op jit(solution)/shard_map/ppermute | solution.py:103
  290.3 1.0 copy-done.8
  291.3 28.3 %collective-permute-done.9 = bf16[192,3072]{1,0:T(8,128)(2,1)} collective-permute-done((bf16[192,3072]{1,0:T(8,128)(2,1)S(1)}, bf16[192,3072]{1,0:T(8,128)(2,1)}, u32[]{:S(2)}, u32[]{:S(2)}) %collective-permute-start.9) | collective-permute-done | bytes 1179680 | tf_op jit(solution)/shard_map/ppermute | solution.py:103
  319.6 27.6 %collective-permute-done.10 = bf16[192,3072]{1,0:T(8,128)(2,1)} collective-permute-done((bf16[192,3072]{1,0:T(8,128)(2,1)}, bf16[192,3072]{1,0:T(8,128)(2,1)}, u32[]{:S(2)}, u32[]{:S(2)}) %collective-permute-start.10) | collective-permute-done | bytes 1179680 | tf_op jit(solution)/shard_map/ppermute | solution.py:103
  347.2 1.3 constant_dynamic-update-slice_fusion.15
  348.5 1.4 constant_dynamic-update-slice_fusion.14
  350.2 1.1 copy-done.5
  351.6 1.3 constant_dynamic-update-slice_fusion.7
  353.0 1.3 constant_dynamic-update-slice_fusion.6
  354.9 1.0 copy-done.14
  355.8 2.7 fusion.9
  358.5 5.1 %copy-done.1 = bf16[3072,3072]{1,0:T(8,128)(2,1)} copy-done((bf16[3072,3072]{1,0:T(8,128)(2,1)}, bf16[3072,3072]{1,0:T(8,128)(2,1)S(1)}, u32[]{:S(2)}) %copy-start.1) | copy-done | bytes 18874392
  363.6 2.0 convolution_bitcast_fusion
  365.6 2.6 copy.39
  368.3 1.9 stack.20
  370.1 1.9 fusion.52
  372.1 1.4 copy-done.15
  373.5 4.8 %fusion.25 = f32[384,12,128]{2,0,1:T(8,128)} fusion(f32[12,128,384]{1,2,0:T(8,128)S(1)} %fusion.52, bf16[128,12,128]{2,1,0:T(8,128)(2,1)S(1)} %copy-done.18, f32[12,128,384]{1,2,0:T(8,128)} %copy-done.21, f32[12,128]{1,0:T(8,128)S(1)} %get-tuple-element.30), kind=kOutput, calls=%fused_computation.22 | convolution fusion | flops 155125632 | bytes 7477248 | tf_op jit(solution)/shard_map/hqk,qhd->khd/dot_general | solution.py:87
  378.3 3.2 copy.37
  381.4 1.9 stack.19
  383.3 2.1 constant_dynamic-update-slice_fusion.17
  386.0 1.0 convert.12
  387.3 1.3 collective-permute-start.11
  388.6 1.5 collective-permute-start.12
  390.3 7.6 %fusion.6 = bf16[128,3072]{1,0:T(8,128)(2,1)} fusion(bf16[128,1536]{0,1:T(8,128)(2,1)S(1)} %bitcast.50, bf16[3072,3072]{1,0:T(8,128)(2,1)} %copy-done.1, s32[]{:T(128)S(6)} %select_n.52), kind=kOutput, calls=%fused_computation.7 | convolution fusion | flops 1208352768 | bytes 10616836 | tf_op jit(solution)/shard_map/dot_general | solution.py:130
  398.7 9.5 %reduce-scatter.3.cloned.1.call-done = bf16[192,3072]{1,0:T(8,128)(2,1)} async-done(((bf16[1536,3072]{1,0:T(8,128)(2,1)}), bf16[192,3072]{1,0:T(8,128)(2,1)}) %reduce-scatter.3.cloned.1.call-update) | async-done | bytes 1179664 | tf_op jit(solution)/shard_map/reduce_scatter | solution.py:134
  408.2 1.0 fusion.75
  409.3 1.2 fusion.78
  410.4 1.4 collective-permute-start.13
  411.8 1.3 collective-permute-start.14
  413.1 5.9 %fusion.31 = bf16[128,12,128]{0,2,1:T(8,128)(2,1)} fusion(bf16[384,12,128]{0,2,1:T(8,128)(2,1)} %copy-done.10, f32[12,128,384]{1,2,0:T(8,128)} %copy-done.15, f32[12,128,384]{1,2,0:T(8,128)} %copy-done.21, f32[12,128]{1,0:T(8,128)S(1)} %get-tuple-element.30), kind=kOutput, calls=%fused_computation.26 | convolution fusion | flops 155322240 | bytes 6297600 | tf_op jit(solution)/shard_map/hqk,khd->qhd/dot_general | solution.py:84
  418.9 2.2 copy.35
  421.1 2.0 reshape.131
  423.1 2.4 reshape.128
  426.3 1.5 slice_add_fusion.1
  428.3 1.2 slice_bitcast_fusion
  429.5 8.7 %reduce-scatter.5.cloned.1.call-done = bf16[192,768]{1,0:T(8,128)(2,1)} async-done(((bf16[192,3072]{1,0:T(8,128)(2,1)}), bf16[192,768]{1,0:T(8,128)(2,1)}) %reduce-scatter.5.cloned.1.call-update) | async-done | bytes 294928 | tf_op jit(solution)/shard_map/reduce_scatter | solution.py:142
  438.2 1.8 convert_element_type.79
  (84 shorter events, 12.0 us)
Async XLA Ops:
  7.2 12.1 %copy-start.11 = (bf16[4,8,4,1536]{3,2,1,0:T(4,128)(2,1)S(1)}, bf16[4,8,4,1536]{3,2,1,0:T(4,128)(2,1)}, u32[]{:S(2)}) copy-start(bf16[4,8,4,1536]{3,2,1,0:T(4,128)(2,1)} %param.8) | copy-start | bytes 1179652
  7.2 12.1 %copy-start.12 = (bf16[4,8,4,1536]{3,2,1,0:T(4,128)(2,1)S(1)}, bf16[4,8,4,1536]{3,2,1,0:T(4,128)(2,1)}, u32[]{:S(2)}) copy-start(bf16[4,8,4,1536]{3,2,1,0:T(4,128)(2,1)} %param.9) | copy-start | bytes 1179652
  7.2 401.0 %reduce-scatter.3.cloned.1.call-start = ((), (), s32[]{:S(2)}) async-start(), calls=%async_computation.2 | async-start | bytes 10616832 | tf_op jit(solution)/shard_map/reduce_scatter | solution.py:134
  9.1 20.6 %copy-start.19 = (bf16[4,8,4,1536]{3,2,1,0:T(4,128)(2,1)S(1)}, bf16[4,8,4,1536]{3,2,1,0:T(4,128)(2,1)}, u32[]{:S(2)}) copy-start(bf16[4,8,4,1536]{3,2,1,0:T(4,128)(2,1)} %param.7) | copy-start | bytes 1179652
  9.1 10.1 %collective-permute-start = (bf16[2,8,4,2,1536]{4,2,1,0,3:T(4,128)(2,1)S(1)}, bf16[2,8,4,2,1536]{4,2,1,0,3:T(4,128)(2,1)S(1)}, u32[]{:S(2)}, u32[]{:S(2)}) collective-permute-start(bf16[2,8,4,2,1536]{4,2,1,0,3:T(4,128)(2,1)S(1)} %get-tuple-element.26), channel_id=1, source_target_pairs={{0,8},{8,16},{16,24},{1,9},{9,17},{17,25},{2,10},{10,18},{18,26},{... | collective-permute-start | bytes 1179656 | tf_op jit(solution)/shard_map/ppermute | solution.py:18
  11.6 7.6 %collective-permute-start.1 = (bf16[2,8,4,2,1536]{4,2,1,0,3:T(4,128)(2,1)S(1)}, bf16[2,8,4,2,1536]{4,2,1,0,3:T(4,128)(2,1)S(1)}, u32[]{:S(2)}, u32[]{:S(2)}) collective-permute-start(bf16[2,8,4,2,1536]{4,2,1,0,3:T(4,128)(2,1)S(1)} %get-tuple-element.27), channel_id=1, source_target_pairs={{8,0},{16,8},{24,16},{9,1},{17,9},{25,17},{10,2},{18,10},{26,18},{... | collective-permute-start | bytes 1179656 | tf_op jit(solution)/shard_map/ppermute | solution.py:19
  15.3 40.3 %copy-start.13 = (bf16[128,3072]{1,0:T(8,128)(2,1)}, bf16[128,3072]{1,0:T(8,128)(2,1)S(1)}, u32[]{:S(2)}) copy-start(bf16[128,3072]{1,0:T(8,128)(2,1)S(1)} %reshape.129) | copy-start | bytes 2359300
  20.6 20.2 %collective-permute-start.2 = (bf16[8,2,4,2,1536]{4,2,1,0,3:T(4,128)(2,1)}, bf16[8,2,4,2,1536]{4,2,1,0,3:T(4,128)(2,1)S(1)}, u32[]{:S(2)}, u32[]{:S(2)}) collective-permute-start(bf16[8,2,4,2,1536]{4,2,1,0,3:T(4,128)(2,1)} %get-tuple-element.22), channel_id=1, source_target_pairs={{0,1},{1,2},{2,3},{3,4},{4,5},{5,6},{6,7},{8,9},{9,10},{10,11},{11... | collective-permute-start | bytes 1179656 | tf_op jit(solution)/shard_map/ppermute | solution.py:18
  24.9 15.9 %collective-permute-start.3 = (bf16[8,2,4,2,1536]{4,2,1,0,3:T(4,128)(2,1)S(1)}, bf16[8,2,4,2,1536]{4,2,1,0,3:T(4,128)(2,1)}, u32[]{:S(2)}, u32[]{:S(2)}) collective-permute-start(bf16[8,2,4,2,1536]{4,2,1,0,3:T(4,128)(2,1)S(1)} %get-tuple-element.23), channel_id=1, source_target_pairs={{1,0},{2,1},{3,2},{4,3},{5,4},{6,5},{7,6},{9,8},{10,9},{11,10},{12... | collective-permute-start | bytes 1179656 | tf_op jit(solution)/shard_map/ppermute | solution.py:19
  48.1 5.1 %copy-start.10 = (bf16[384,12,128]{0,2,1:T(8,128)(2,1)}, bf16[384,12,128]{0,2,1:T(8,128)(2,1)S(1)}, u32[]{:S(2)}) copy-start(bf16[384,12,128]{0,2,1:T(8,128)(2,1)S(1)} %copy.33) | copy-start | bytes 3538948
  51.2 2.9 copy-start.2
  51.2 2.0 copy-start.20
  54.1 1.5 copy-start.21
  55.6 5.1 %copy-start.16 = (bf16[12,128,128]{2,1,0:T(8,128)(2,1)}, bf16[12,128,128]{2,1,0:T(8,128)(2,1)S(1)}, u32[]{:S(2)}) copy-start(bf16[12,128,128]{2,1,0:T(8,128)(2,1)S(1)} %convolution_convert_fusion.1) | copy-start | bytes 1179652
  60.6 1.3 copy-start.3
  60.6 377.5 %reduce-scatter.5.cloned.1.call-start = ((), (), s32[]{:S(2)}) async-start(), calls=%async_computation.3 | async-start | bytes 1474560 | tf_op jit(solution)/shard_map/reduce_scatter | solution.py:142
  61.9 50.6 %collective-permute-start.4 = (bf16[192,3072]{1,0:T(8,128)(2,1)S(1)}, bf16[192,3072]{1,0:T(8,128)(2,1)S(1)}, u32[]{:S(2)}, u32[]{:S(2)}) collective-permute-start(bf16[192,3072]{1,0:T(8,128)(2,1)S(1)} %copy-done.3), channel_id=1, source_target_pairs={{0,1},{1,2},{2,3},{3,4},{4,5},{5,6},{6,7},{7,0},{8,9},{9,10},{10,1... | collective-permute-start | bytes 3538952 | tf_op jit(solution)/shard_map/ppermute | solution.py:103
  112.5 56.4 %collective-permute-start.5 = (bf16[192,3072]{1,0:T(8,128)(2,1)S(1)}, bf16[192,3072]{1,0:T(8,128)(2,1)S(1)}, u32[]{:S(2)}, u32[]{:S(2)}) collective-permute-start(bf16[192,3072]{1,0:T(8,128)(2,1)S(1)} %collective-permute-done.4), channel_id=1, source_target_pairs={{0,1},{1,2},{2,3},{3,4},{4,5},{5,6},{6,7},{7,0},{8,9},{9,10},{10,1... | collective-permute-start | bytes 3538952 | tf_op jit(solution)/shard_map/ppermute | solution.py:103
  168.9 52.6 %collective-permute-start.6 = (bf16[192,3072]{1,0:T(8,128)(2,1)S(1)}, bf16[192,3072]{1,0:T(8,128)(2,1)S(1)}, u32[]{:S(2)}, u32[]{:S(2)}) collective-permute-start(bf16[192,3072]{1,0:T(8,128)(2,1)S(1)} %collective-permute-done.5), channel_id=1, source_target_pairs={{0,1},{1,2},{2,3},{3,4},{4,5},{5,6},{6,7},{7,0},{8,9},{9,10},{10,1... | collective-permute-start | bytes 3538952 | tf_op jit(solution)/shard_map/ppermute | solution.py:103
  221.6 1.0 copy-start.4
  222.6 37.5 %collective-permute-start.7 = (bf16[192,3072]{1,0:T(8,128)(2,1)S(1)}, bf16[192,3072]{1,0:T(8,128)(2,1)S(1)}, u32[]{:S(2)}, u32[]{:S(2)}) collective-permute-start(bf16[192,3072]{1,0:T(8,128)(2,1)S(1)} %collective-permute-done.6), channel_id=1, source_target_pairs={{0,1},{1,2},{2,3},{3,4},{4,5},{5,6},{6,7},{7,0},{8,9},{9,10},{10,1... | collective-permute-start | bytes 3538952 | tf_op jit(solution)/shard_map/ppermute | solution.py:103
  260.1 1.0 copy-start.6
  261.1 29.2 %collective-permute-start.8 = (bf16[192,3072]{1,0:T(8,128)(2,1)S(1)}, bf16[192,3072]{1,0:T(8,128)(2,1)S(1)}, u32[]{:S(2)}, u32[]{:S(2)}) collective-permute-start(bf16[192,3072]{1,0:T(8,128)(2,1)S(1)} %collective-permute-done.7), channel_id=1, source_target_pairs={{0,1},{1,2},{2,3},{3,4},{4,5},{5,6},{6,7},{7,0},{8,9},{9,10},{10,1... | collective-permute-start | bytes 3538952 | tf_op jit(solution)/shard_map/ppermute | solution.py:103
  290.3 1.0 copy-start.8
  291.3 28.3 %collective-permute-start.9 = (bf16[192,3072]{1,0:T(8,128)(2,1)S(1)}, bf16[192,3072]{1,0:T(8,128)(2,1)}, u32[]{:S(2)}, u32[]{:S(2)}) collective-permute-start(bf16[192,3072]{1,0:T(8,128)(2,1)S(1)} %collective-permute-done.8), channel_id=1, source_target_pairs={{0,1},{1,2},{2,3},{3,4},{4,5},{5,6},{6,7},{7,0},{8,9},{9,10},{10,1... | collective-permute-start | bytes 3538952 | tf_op jit(solution)/shard_map/ppermute | solution.py:103
  319.6 27.6 %collective-permute-start.10 = (bf16[192,3072]{1,0:T(8,128)(2,1)}, bf16[192,3072]{1,0:T(8,128)(2,1)}, u32[]{:S(2)}, u32[]{:S(2)}) collective-permute-start(bf16[192,3072]{1,0:T(8,128)(2,1)} %collective-permute-done.9), channel_id=1, source_target_pairs={{0,1},{1,2},{2,3},{3,4},{4,5},{5,6},{6,7},{7,0},{8,9},{9,10},{10,1... | collective-permute-start | bytes 3538952 | tf_op jit(solution)/shard_map/ppermute | solution.py:103
  319.6 30.4 %copy-start.9 = (bf16[192,3072]{1,0:T(8,128)(2,1)S(1)}, bf16[192,3072]{1,0:T(8,128)(2,1)}, u32[]{:S(2)}) copy-start(bf16[192,3072]{1,0:T(8,128)(2,1)} %copy-done.8) | copy-start | bytes 3538948
  348.5 1.6 copy-start.7
  350.0 1.3 copy-start.5
  354.7 1.1 copy-start.14
  355.8 7.8 %copy-start.1 = (bf16[3072,3072]{1,0:T(8,128)(2,1)}, bf16[3072,3072]{1,0:T(8,128)(2,1)S(1)}, u32[]{:S(2)}) copy-start(bf16[3072,3072]{1,0:T(8,128)(2,1)S(1)} %constant_dynamic-update-slice_fusion) | copy-start | bytes 56623108
  355.8 7.8 %copy-start.22 = (f32[12,128,384]{1,2,0:T(8,128)S(1)}, f32[12,128,384]{1,2,0:T(8,128)}, u32[]{:S(2)}) copy-start(f32[12,128,384]{1,2,0:T(8,128)} %copy-done.21) | copy-start | bytes 7077892
  370.1 3.3 copy-start.18
  372.1 1.4 copy-start.15
  383.3 2.4 copy-start
  387.0 3.3 copy-start.17
  387.3 10.6 %collective-permute-start.11 = (bf16[8,2,4,2,1536]{4,2,1,0,3:T(4,128)(2,1)S(1)}, bf16[8,2,4,2,1536]{4,2,1,0,3:T(4,128)(2,1)S(1)}, u32[]{:S(2)}, u32[]{:S(2)}) collective-permute-start(bf16[8,2,4,2,1536]{4,2,1,0,3:T(4,128)(2,1)S(1)} %get-tuple-element.16), channel_id=1, source_target_pairs={{0,1},{1,2},{2,3},{3,4},{4,5},{5,6},{6,7},{8,9},{9,10},{10,11},{11... | collective-permute-start | bytes 1179656 | tf_op jit(solution)/shard_map/ppermute | solution.py:27
  388.6 9.7 %collective-permute-start.12 = (bf16[8,2,4,2,1536]{4,2,1,0,3:T(4,128)(2,1)S(1)}, bf16[8,2,4,2,1536]{4,2,1,0,3:T(4,128)(2,1)S(1)}, u32[]{:S(2)}, u32[]{:S(2)}) collective-permute-start(bf16[8,2,4,2,1536]{4,2,1,0,3:T(4,128)(2,1)S(1)} %get-tuple-element.17), channel_id=1, source_target_pairs={{1,0},{2,1},{3,2},{4,3},{5,4},{6,5},{7,6},{9,8},{10,9},{11,10},{12... | collective-permute-start | bytes 1179656 | tf_op jit(solution)/shard_map/ppermute | solution.py:27
  410.4 15.9 %collective-permute-start.13 = (bf16[2,8,4,2,1536]{4,2,1,0,3:T(4,128)(2,1)}, bf16[2,8,4,2,1536]{4,2,1,0,3:T(4,128)(2,1)S(1)}, u32[]{:S(2)}, u32[]{:S(2)}) collective-permute-start(bf16[2,8,4,2,1536]{4,2,1,0,3:T(4,128)(2,1)} %get-tuple-element.20), channel_id=1, source_target_pairs={{0,8},{8,16},{16,24},{1,9},{9,17},{17,25},{2,10},{10,18},{18,26},{... | collective-permute-start | bytes 1179656 | tf_op jit(solution)/shard_map/ppermute | solution.py:27
  411.8 14.5 %collective-permute-start.14 = (bf16[2,8,4,2,1536]{4,2,1,0,3:T(4,128)(2,1)}, bf16[2,8,4,2,1536]{4,2,1,0,3:T(4,128)(2,1)}, u32[]{:S(2)}, u32[]{:S(2)}) collective-permute-start(bf16[2,8,4,2,1536]{4,2,1,0,3:T(4,128)(2,1)} %get-tuple-element.21), channel_id=1, source_target_pairs={{8,0},{16,8},{24,16},{9,1},{17,9},{25,17},{10,2},{18,10},{26,18},{... | collective-permute-start | bytes 1179656 | tf_op jit(solution)/shard_map/ppermute | solution.py:27
Sparse Core Ops, SparseCore 0:
  60.8 347.4 reduce-scatter.2
  410.8 27.3 reduce-scatter.4
